TPU v7x, 32 devices: a whole 2x2x4 slice. The times are simulated.
32 devices in a mesh: gx: 2 (over x), gy: 4 (over y, core), gz: 4 (over z).
Axes of the slice: x: 2, y: 2, z: 4, core: 2. Of those that a mesh axis runs over, the one named last changes fastest.
Arguments:
- conserved: float32 [5, 16, 32, 256], P(None, 'gz', 'gy', 'gx'), may hold values from -3 to 12, as said below
- metrics: float32 [9, 16, 32, 256], P(None, 'gz', 'gy', 'gx'), may hold values from -0.6 to 2, as said below
- inv_volume: float32 [16, 32, 256], P('gz', 'gy', 'gx'), may hold values from 0.5 to 2
- wake_donor: int32 [256], P('gx'), may hold values from -1 to 255, as said below
Outputs:
- section_state: float32 [5, 16, 32, 256], P(None, 'gz', 'gy', 'gx')
- time_rate: float32 [5, 16, 32, 256], P(None, 'gz', 'gy', 'gx')
Inputs may be any that keep to these rules, and one draw needn't show every extreme that they name: `conserved`: each cell holds density rho of 0.5 to 2, pressure p of 0.5 to 2 and velocity components u of -1.5 to 1.5 as (rho, rho u, p / 0.4 + rho |u|^2 / 2). `metrics`: in each cell, row d (entries 3 d to 3 d + 2) has its entry 3 d + d between 0.5 and 2 and its other two entries at most 0.3 times that entry in magnitude. wake_donor[i] is either 256 - 1 - i or -1, and wake_donor[i] >= 0 exactly where wake_donor[255 - i] >= 0.
All inputs are finite; a program needn't handle non-finite values.
Results may differ from a plain program's by a relative error of at most 0.0001.
Values sent between devices are 32-bit elements; how exact they have to be, the bound alone decides.
A program may use at most 64 MiB of HBM per device.

v0:
```python
import jax
import jax.numpy as jnp
from jax import lax
from jax.sharding import PartitionSpec as P

GAMMA = 1.4
WENO_EPS = 1e-06
STEP_SIZE = 0.08


def from_partner(x, axis, bit):
    return lax.ppermute(x, axis, [(i, i ^ 1 << bit) for i in range(lax.axis_size(axis))])


def padded(block, sides, width, periodic):
    for axis, dim in sides:
        count = lax.axis_size(axis)
        forward = [(i, i + 1) for i in range(count - 1)]
        if periodic:
            forward.append((count - 1, 0))
        backward = [(target, source) for source, target in forward]
        low = lax.ppermute(
            lax.slice_in_dim(block, block.shape[dim] - width, None, axis=dim), axis, forward
        )
        high = lax.ppermute(lax.slice_in_dim(block, 0, width, axis=dim), axis, backward)
        block = jnp.concatenate([low, block, high], axis=dim)
    return block


def slab_of(values, start, amount, axis):
    return lax.slice_in_dim(values, start, start + amount, axis=values.ndim + axis)


def cross_of(first, second):
    return [
        first[1] * second[2] - first[2] * second[1],
        first[2] * second[0] - first[0] * second[2],
        first[0] * second[1] - first[1] * second[0],
    ]


def inner_of(first, second):
    return first[0] * second[0] + first[1] * second[1] + first[2] * second[2]


def cell_terms(fields, metric_row):
    density = fields[0]
    velocity = fields[1:4] / density
    kinetic = 0.5 * jnp.sum(fields[1:4] * velocity, axis=0)
    pressure = (GAMMA - 1.0) * (fields[4] - kinetic)
    contra = jnp.sum(metric_row * velocity, axis=0)
    fluxes = jnp.stack(
        [
            fields[0] * contra,
            fields[1] * contra + metric_row[0] * pressure,
            fields[2] * contra + metric_row[1] * pressure,
            fields[3] * contra + metric_row[2] * pressure,
            (fields[4] + pressure) * contra,
        ]
    )
    sound_speed = jnp.sqrt(GAMMA * pressure / density)
    speeds = jnp.abs(contra) + sound_speed * jnp.sqrt(jnp.sum(metric_row * metric_row, axis=0))
    primitive = jnp.concatenate([density[None], velocity, pressure[None]], axis=0)
    return (primitive, fluxes, speeds)


def eigen_pair(state, metric_row, pick):
    density = state[0]
    velocity = [state[1], state[2], state[3]]
    pressure = state[4]
    row_size = jnp.sqrt(metric_row[0] ** 2 + metric_row[1] ** 2 + metric_row[2] ** 2)
    normal = [metric_row[member] / row_size for member in range(3)]
    axis_unit = [1.0 if member == pick else 0.0 for member in range(3)]
    raw_cross = cross_of(normal, axis_unit)
    raw_size = jnp.sqrt(raw_cross[0] ** 2 + raw_cross[1] ** 2 + raw_cross[2] ** 2)
    tangent = [raw_cross[member] / raw_size for member in range(3)]
    binormal = cross_of(normal, tangent)
    sound_speed = jnp.sqrt(GAMMA * pressure / density)
    inverse = 1.0 / sound_speed
    kinetic = 0.5 * inner_of(velocity, velocity)
    enthalpy = GAMMA / (GAMMA - 1.0) * pressure / density + kinetic
    normal_speed = inner_of(normal, velocity)
    tangent_speed = inner_of(tangent, velocity)
    binormal_speed = inner_of(binormal, velocity)
    factor = (GAMMA - 1.0) * inverse * inverse
    scaled = factor * kinetic
    left_rows = [
        [0.5 * (scaled + normal_speed * inverse)]
        + [0.5 * (-factor * velocity[member] - normal[member] * inverse) for member in range(3)]
        + [0.5 * factor],
        [1.0 - scaled] + [factor * velocity[member] for member in range(3)] + [-factor],
        [-tangent_speed] + tangent + [0.0],
        [-binormal_speed] + binormal + [0.0],
        [0.5 * (scaled - normal_speed * inverse)]
        + [0.5 * (-factor * velocity[member] + normal[member] * inverse) for member in range(3)]
        + [0.5 * factor],
    ]
    right_columns = [
        [1.0]
        + [velocity[member] - sound_speed * normal[member] for member in range(3)]
        + [enthalpy - sound_speed * normal_speed],
        [1.0] + velocity + [kinetic],
        [0.0] + tangent + [tangent_speed],
        [0.0] + binormal + [binormal_speed],
        [1.0]
        + [velocity[member] + sound_speed * normal[member] for member in range(3)]
        + [enthalpy + sound_speed * normal_speed],
    ]
    return (left_rows, right_columns)


def project_left(matrix, vector):
    return jnp.stack(
        [
            sum((matrix[member][second] * vector[second] for second in range(5)))
            for member in range(5)
        ]
    )


def apply_right(matrix, vector):
    return jnp.stack(
        [
            sum((matrix[second][member] * vector[second] for second in range(5)))
            for member in range(5)
        ]
    )


def weno_side(stencil):
    far_left, near_left, center, near_right, far_right = stencil
    guess_zero = (2.0 * far_left - 7.0 * near_left + 11.0 * center) / 6.0
    guess_one = (-near_left + 5.0 * center + 2.0 * near_right) / 6.0
    guess_two = (2.0 * center + 5.0 * near_right - far_right) / 6.0
    smooth_zero = (
        13.0 / 12.0 * (far_left - 2.0 * near_left + center) ** 2
        + 0.25 * (far_left - 4.0 * near_left + 3.0 * center) ** 2
    )
    smooth_one = (
        13.0 / 12.0 * (near_left - 2.0 * center + near_right) ** 2
        + 0.25 * (near_left - near_right) ** 2
    )
    smooth_two = (
        13.0 / 12.0 * (center - 2.0 * near_right + far_right) ** 2
        + 0.25 * (3.0 * center - 4.0 * near_right + far_right) ** 2
    )
    weight_zero = 0.1 / (WENO_EPS + smooth_zero) ** 2
    weight_one = 0.6 / (WENO_EPS + smooth_one) ** 2
    weight_two = 0.3 / (WENO_EPS + smooth_two) ** 2
    return (weight_zero * guess_zero + weight_one * guess_one + weight_two * guess_two) / (
        weight_zero + weight_one + weight_two
    )


def interface_flux(fields, metric_row, axis, pick):
    primitive, fluxes, speeds = cell_terms(fields, metric_row)
    faces_count = fields.shape[fields.ndim + axis] - 5
    mean_state = 0.5 * (
        slab_of(primitive, 2, faces_count, axis) + slab_of(primitive, 3, faces_count, axis)
    )
    mean_row = 0.5 * (
        slab_of(metric_row, 2, faces_count, axis) + slab_of(metric_row, 3, faces_count, axis)
    )
    left_rows, right_columns = eigen_pair(mean_state, mean_row, pick)
    max_speed = slab_of(speeds, 0, faces_count, axis)
    for offset in range(1, 6):
        max_speed = jnp.maximum(max_speed, slab_of(speeds, offset, faces_count, axis))
    upwind = []
    downwind = []
    for offset in range(6):
        state_chars = project_left(left_rows, slab_of(fields, offset, faces_count, axis))
        flux_chars = project_left(left_rows, slab_of(fluxes, offset, faces_count, axis))
        upwind.append(0.5 * (flux_chars + max_speed * state_chars))
        downwind.append(0.5 * (flux_chars - max_speed * state_chars))
    combined = weno_side(upwind[0:5]) + weno_side(downwind[5:0:-1])
    return apply_right(right_columns, combined)


def divergence(fields, metric_row, axis, pick):
    face_flux = interface_flux(fields, metric_row, axis, pick)
    cells_count = face_flux.shape[face_flux.ndim + axis] - 1
    return slab_of(face_flux, 1, cells_count, axis) - slab_of(face_flux, 0, cells_count, axis)


def fix_ends(extended, at_start, at_end):
    interior = extended[..., 3:-3]
    lower_ghost = jnp.where(at_start, jnp.repeat(interior[..., :1], 3, axis=-1), extended[..., :3])
    upper_ghost = jnp.where(at_end, jnp.repeat(interior[..., -1:], 3, axis=-1), extended[..., -3:])
    return jnp.concatenate([lower_ghost, interior, upper_ghost], axis=-1)


def fix_wall(extended, ghosts, at_start, at_end):
    interior = extended[:, :, 3:-3, :]
    lower_ghost = jnp.where(at_start, ghosts, extended[:, :, :3, :])
    upper_ghost = jnp.where(
        at_end, jnp.repeat(interior[:, :, -1:, :], 3, axis=2), extended[:, :, -3:, :]
    )
    return jnp.concatenate([lower_ghost, interior, upper_ghost], axis=2)


def local(conserved, metrics, inv_volume, wake_donor):
    at_inflow = lax.axis_index("gx") == 0
    at_outflow = lax.axis_index("gx") == lax.axis_size("gx") - 1
    at_wall = lax.axis_index("gy") == 0
    at_top = lax.axis_index("gy") == lax.axis_size("gy") - 1
    mirrored = jnp.concatenate([conserved[:, :, 2::-1, :], metrics[3:6, :, 2::-1, :]], axis=0)
    for bit_number in range(lax.axis_size("gx").bit_length() - 1):
        mirrored = from_partner(mirrored, "gx", bit_number)
    mirrored = mirrored[..., ::-1]
    stream_flow, stream_metric = (
        padded(conserved, (("gx", 3),), 3, False),
        padded(metrics, (("gx", 3),), 3, False),
    )
    normal_flow, normal_metric = (
        padded(conserved, (("gy", 2),), 3, False),
        padded(metrics, (("gy", 2),), 3, False),
    )
    span_flow, span_metric = (
        padded(conserved, (("gz", 1),), 3, True),
        padded(metrics, (("gz", 1),), 3, True),
    )
    stream_row = stream_metric[0:3]
    normal_row = normal_metric[3:6]
    span_row = span_metric[6:9]
    stream_flow = fix_ends(stream_flow, at_inflow, at_outflow)
    stream_row = fix_ends(stream_row, at_inflow, at_outflow)
    momentum_sign = jnp.array([1.0, -1.0, -1.0, -1.0, 1.0], dtype=jnp.float32)[:, None, None, None]
    is_wake = wake_donor >= 0
    wake_flow = jnp.where(is_wake, mirrored[0:5], conserved[:, :, 2::-1, :] * momentum_sign)
    wake_row = jnp.where(is_wake, mirrored[5:8], metrics[3:6, :, 2::-1, :])
    normal_flow = fix_wall(normal_flow, wake_flow, at_wall, at_top)
    normal_row = fix_wall(normal_row, wake_row, at_wall, at_top)
    summed = divergence(stream_flow, stream_row, -1, 1)
    summed = summed + divergence(normal_flow, normal_row, -2, 2)
    summed = summed + divergence(span_flow, span_row, -3, 0)
    time_rate = -inv_volume[None] * summed
    return (conserved + STEP_SIZE * time_rate, time_rate)


def solution(mesh):
    placed = (P(None, "gz", "gy", "gx"), P(None, "gz", "gy", "gx"), P("gz", "gy", "gx"), P("gx"))
    return jax.shard_map(
        local,
        mesh=mesh,
        in_specs=placed,
        out_specs=(P(None, "gz", "gy", "gx"), P(None, "gz", "gy", "gx")),
        check_vma=False,
    )
```

profile of v0, /device:TPU:0, one launch (start us, length us, event | category | flops | bytes accessed | tf_op | source)
XLA Modules:
  0.0 47.5 jit_solution(11533834819251356184)
XLA Ops:
  0.6 1.0 %fusion.195 = (f32[5,4,8,3]{3,2,1,0:T(8,128)S(1)}, f32[5,4,8,3]{3,2,1,0:T(8,128)S(1)}) fusion(f32[5,4,8,128]{3,2,1,0:T(8,128)} %param.5), kind=kLoop, calls=%fused_computation.685 | loop fusion | bytes 7680 | tf_op jit(solution)/shard_map/slice | solution.py:25
  1.7 1.3 %collective-permute-start.1 = (f32[5,4,8,3]{3,2,1,0:T(8,128)S(1)}, f32[5,4,8,3]{3,2,1,0:T(8,128)S(1)}, u32[]{:S(2)}, u32[]{:S(2)}) collective-permute-start(f32[5,4,8,3]{3,2,1,0:T(8,128)S(1)} %get-tuple-element.353), channel_id=1, source_target_pairs={{16,0},{17,1},{18,2},{19,3},{20,4},{21,5},{22,6},{23,7},{24,8},{25... | collective-permute-start | bytes 5768 | tf_op jit(solution)/shard_map/ppermute | solution.py:25
  3.0 5.0 %collective-permute-start = (f32[5,4,8,3]{3,2,1,0:T(8,128)S(1)}, f32[5,4,8,3]{3,2,1,0:T(8,128)S(1)}, u32[]{:S(2)}, u32[]{:S(2)}) collective-permute-start(f32[5,4,8,3]{3,2,1,0:T(8,128)S(1)} %get-tuple-element.354), channel_id=1, source_target_pairs={{0,16},{1,17},{2,18},{3,19},{4,20},{5,21},{6,22},{7,23},{8,24},{9,... | collective-permute-start | bytes 5768 | tf_op jit(solution)/shard_map/ppermute | solution.py:22
  8.0 0.1 fusion.191
  8.1 1.3 %collective-permute-start.3 = (f32[9,4,8,3]{3,2,1,0:T(8,128)S(1)}, f32[9,4,8,3]{3,2,1,0:T(8,128)S(1)}, u32[]{:S(2)}, u32[]{:S(2)}) collective-permute-start(f32[9,4,8,3]{3,2,1,0:T(8,128)S(1)} %get-tuple-element.329), channel_id=1, source_target_pairs={{16,0},{17,1},{18,2},{19,3},{20,4},{21,5},{22,6},{23,7},{24,8},{25... | collective-permute-start | bytes 10376 | tf_op jit(solution)/shard_map/ppermute | solution.py:25
  9.4 4.6 %collective-permute-start.2 = (f32[9,4,8,3]{3,2,1,0:T(8,128)S(1)}, f32[9,4,8,3]{3,2,1,0:T(8,128)S(1)}, u32[]{:S(2)}, u32[]{:S(2)}) collective-permute-start(f32[9,4,8,3]{3,2,1,0:T(8,128)S(1)} %get-tuple-element.328), channel_id=1, source_target_pairs={{0,16},{1,17},{2,18},{3,19},{4,20},{5,21},{6,22},{7,23},{8,24},{9,... | collective-permute-start | bytes 10376 | tf_op jit(solution)/shard_map/ppermute | solution.py:22
  14.0 1.3 %collective-permute-start.6 = (f32[5,4,3,128]{3,2,1,0:T(4,128)S(1)}, f32[5,4,3,128]{3,2,1,0:T(4,128)S(1)}, u32[]{:S(2)}, u32[]{:S(2)}) collective-permute-start(f32[5,4,3,128]{3,2,1,0:T(4,128)S(1)} %get-tuple-element.355), channel_id=1, source_target_pairs={{4,0},{8,4},{12,8},{5,1},{9,5},{13,9},{6,2},{10,6},{14,10},{7,3},{... | collective-permute-start | bytes 92168 | tf_op jit(solution)/shard_map/ppermute | solution.py:25
  15.3 0.2 slice_reduce_fusion.1
  15.5 0.2 slice_reduce_fusion.3
  15.9 0.6 %copy-done.4 = s32[128]{0:T(128)S(1)} copy-done((s32[128]{0:T(128)S(1)}, s32[128]{0:T(128)}, u32[]{:S(2)}) %copy-start.4) | copy-done | bytes 536
  16.6 0.7 %copy-done.2 = f32[4,8,128]{2,1,0:T(8,128)S(1)} copy-done((f32[4,8,128]{2,1,0:T(8,128)S(1)}, f32[4,8,128]{2,1,0:T(8,128)}, u32[]{:S(2)}) %copy-start.2) | copy-done | bytes 16408
  17.3 0.1 broadcast_select_fusion
  17.4 3.0 %collective-permute-start.5 = (f32[5,4,3,128]{3,2,1,0:T(4,128)S(1)}, f32[5,4,3,128]{3,2,1,0:T(4,128)S(1)}, u32[]{:S(2)}, u32[]{:S(2)}) collective-permute-start(f32[5,4,3,128]{3,2,1,0:T(4,128)S(1)} %get-tuple-element.356), channel_id=1, source_target_pairs={{0,4},{4,8},{8,12},{1,5},{5,9},{9,13},{2,6},{6,10},{10,14},{3,7},{... | collective-permute-start | bytes 92168 | tf_op jit(solution)/shard_map/ppermute | solution.py:22
  20.4 0.1 broadcast_select_fusion.1
  20.5 0.1 pad_maximum_fusion.1
  20.7 4.2 %collective-permute-start.7 = (f32[9,4,3,128]{3,2,1,0:T(4,128)S(1)}, f32[9,4,3,128]{3,2,1,0:T(4,128)S(1)}, u32[]{:S(2)}, u32[]{:S(2)}) collective-permute-start(f32[9,4,3,128]{3,2,1,0:T(4,128)S(1)} %get-tuple-element.332), channel_id=1, source_target_pairs={{0,4},{4,8},{8,12},{1,5},{5,9},{9,13},{2,6},{6,10},{10,14},{3,7},{... | collective-permute-start | bytes 165896 | tf_op jit(solution)/shard_map/ppermute | solution.py:22
  24.9 0.1 slice_select_fusion
  25.0 1.3 %collective-permute-start.8 = (f32[9,4,3,128]{3,2,1,0:T(4,128)S(1)}, f32[9,4,3,128]{3,2,1,0:T(4,128)S(1)}, u32[]{:S(2)}, u32[]{:S(2)}) collective-permute-start(f32[9,4,3,128]{3,2,1,0:T(4,128)S(1)} %get-tuple-element.333), channel_id=1, source_target_pairs={{4,0},{8,4},{12,8},{5,1},{9,5},{13,9},{6,2},{10,6},{14,10},{7,3},{... | collective-permute-start | bytes 165896 | tf_op jit(solution)/shard_map/ppermute | solution.py:25
  26.3 0.1 slice_select_fusion.1
  26.4 0.1 fusion.15
  26.5 0.1 multiply_reduce_fusion.6
  26.7 0.1 fusion.1
  26.8 0.1 constant_dynamic-update-slice_fusion.9
  27.0 0.1 constant_dynamic-update-slice_fusion.29
  27.1 0.1 constant_dynamic-update-slice_fusion.49
  27.3 0.1 constant_dynamic-update-slice_fusion.19
  27.4 0.1 constant_dynamic-update-slice_fusion.59
  27.6 0.2 constant_dynamic-update-slice_fusion.44
  27.7 0.1 constant_dynamic-update-slice_fusion.4
  27.8 0.2 constant_dynamic-update-slice_fusion.24
  28.0 0.1 slice_maximum_fusion.5
  28.2 0.1 constant_dynamic-update-slice_fusion.7
  28.8 0.2 constant_dynamic-update-slice_fusion.43
  29.0 0.1 constant_dynamic-update-slice_fusion.3
  29.1 0.2 constant_dynamic-update-slice_fusion.52
  29.3 0.1 constant_dynamic-update-slice_fusion.2
  29.4 0.1 constant_dynamic-update-slice_fusion.1
  29.5 0.1 constant_dynamic-update-slice_fusion
  29.6 0.2 constant_dynamic-update-slice_fusion.41
  29.8 0.2 constant_dynamic-update-slice_fusion.40
  30.0 0.2 constant_dynamic-update-slice_fusion.23
  30.1 0.2 constant_dynamic-update-slice_fusion.22
  30.3 0.2 constant_dynamic-update-slice_fusion.21
  30.4 0.2 constant_dynamic-update-slice_fusion.20
  30.6 0.8 %divide_add_fusion.1 = f32[5,4,8,129]{3,2,1,0:T(8,128)S(1)} fusion(f32[5,4,8,129]{3,2,1,0:T(8,128)S(1)} %get-tuple-element.203, f32[5,4,8,129]{3,2,1,0:T(8,128)S(1)} %get-tuple-element.202, f32[5,4,8,129]{3,2,1,0:T(8,128)S(1)} %get-tuple-element.197, f32[5,4,8,129]{3,2,1,0:T(8,128)S(1)} %get-tuple-element.196, f32[5,4,8,129]{3,2,1,0:T(8,128)S(1)} %get-tuple-element.191, ...), kind=kLoop, calls=%fused_computation.333 | loop fusion | flops 3034080 | bytes 1089792 | tf_op jit(solution)/shard_map/add | solution.py:175
  31.6 1.6 %collective-permute-start.9 = (f32[5,3,8,128]{3,2,1,0:T(8,128)S(1)}, f32[5,3,8,128]{3,2,1,0:T(8,128)S(1)}, u32[]{:S(2)}, u32[]{:S(2)}) collective-permute-start(f32[5,3,8,128]{3,2,1,0:T(8,128)S(1)} %get-tuple-element.361), channel_id=1, source_target_pairs={{0,1},{1,2},{2,3},{3,0},{4,5},{5,6},{6,7},{7,4},{8,9},{9,10},{10,1... | collective-permute-start | bytes 184328 | tf_op jit(solution)/shard_map/ppermute | solution.py:22
  33.3 2.3 %collective-permute-start.10 = (f32[5,3,8,128]{3,2,1,0:T(8,128)S(1)}, f32[5,3,8,128]{3,2,1,0:T(8,128)S(1)}, u32[]{:S(2)}, u32[]{:S(2)}) collective-permute-start(f32[5,3,8,128]{3,2,1,0:T(8,128)S(1)} %get-tuple-element.360), channel_id=1, source_target_pairs={{1,0},{2,1},{3,2},{0,3},{5,4},{6,5},{7,6},{4,7},{9,8},{10,9},{11,1... | collective-permute-start | bytes 184328 | tf_op jit(solution)/shard_map/ppermute | solution.py:25
  35.6 0.1 slice.1065
  35.7 0.1 collective-permute-start.11
  35.8 0.6 %copy-done.3 = f32[5]{0:T(128)S(1)} copy-done((f32[5]{0:T(128)S(1)}, f32[5]{0:T(128)}, u32[]{:S(2)}) %copy-start.3) | copy-done | bytes 44
  36.4 0.1 select_select_fusion
  36.5 0.1 slice.1080
  36.6 3.3 %collective-permute-start.12 = (f32[9,3,8,128]{3,2,1,0:T(8,128)S(1)}, f32[9,3,8,128]{3,2,1,0:T(8,128)S(1)}, u32[]{:S(2)}, u32[]{:S(2)}) collective-permute-start(f32[9,3,8,128]{3,2,1,0:T(8,128)S(1)} %get-tuple-element.334), channel_id=1, source_target_pairs={{1,0},{2,1},{3,2},{0,3},{5,4},{6,5},{7,6},{4,7},{9,8},{10,9},{11,1... | collective-permute-start | bytes 331784 | tf_op jit(solution)/shard_map/ppermute | solution.py:25
  40.2 0.1 constant_dynamic-update-slice_fusion.74
  40.6 0.1 constant_dynamic-update-slice_fusion.109
  40.7 0.1 constant_dynamic-update-slice_fusion.89
  41.5 0.1 constant_dynamic-update-slice_fusion.108
  41.9 0.1 constant_dynamic-update-slice_fusion.88
  42.2 0.8 %divide_add_fusion = f32[5,4,9,128]{3,2,1,0:T(8,128)S(1)} fusion(f32[5,4,9,128]{3,2,1,0:T(8,128)S(1)} %get-tuple-element.224, f32[5,4,9,128]{3,2,1,0:T(8,128)S(1)} %get-tuple-element.223, f32[5,4,9,128]{3,2,1,0:T(8,128)S(1)} %get-tuple-element.218, f32[5,4,9,128]{3,2,1,0:T(8,128)S(1)} %get-tuple-element.217, f32[5,4,9,128]{3,2,1,0:T(8,128)S(1)} %get-tuple-element.212, ...), kind=kLoop, calls=%fused_computation.326 | loop fusion | flops 3386880 | bytes 1216512 | tf_op jit(solution)/shard_map/add | solution.py:175
  43.3 0.3 collective-permute-done.11
  43.6 1.1 %collective-permute-done.12 = f32[9,3,8,128]{3,2,1,0:T(8,128)S(1)} collective-permute-done((f32[9,3,8,128]{3,2,1,0:T(8,128)S(1)}, f32[9,3,8,128]{3,2,1,0:T(8,128)S(1)}, u32[]{:S(2)}, u32[]{:S(2)}) %collective-permute-start.12) | collective-permute-done | bytes 110624 | tf_op jit(solution)/shard_map/ppermute | solution.py:25
  44.8 0.1 constant_dynamic-update-slice_fusion.147
  46.1 0.5 %divide_add_fusion.2 = f32[5,5,8,128]{3,2,1,0:T(8,128)S(1)} fusion(f32[5,5,8,128]{3,2,1,0:T(8,128)S(1)} %get-tuple-element.245, f32[5,5,8,128]{3,2,1,0:T(8,128)S(1)} %get-tuple-element.244, f32[5,5,8,128]{3,2,1,0:T(8,128)S(1)} %get-tuple-element.239, f32[5,5,8,128]{3,2,1,0:T(8,128)S(1)} %get-tuple-element.238, f32[5,5,8,128]{3,2,1,0:T(8,128)S(1)} %get-tuple-element.233, ...), kind=kLoop, calls=%fused_computation.346 | loop fusion | flops 3763200 | bytes 1351680 | tf_op jit(solution)/shard_map/add | solution.py:175
  46.7 0.8 %multiply_add_fusion = (f32[5,4,8,128]{3,2,1,0:T(8,128)}, f32[5,4,8,128]{3,2,1,0:T(8,128)}) fusion(f32[5,4,8,128]{3,2,1,0:T(8,128)S(1)} %copy-done, f32[5,5,8,128]{3,2,1,0:T(8,128)S(1)} %constant_dynamic-update-slice_fusion.200, f32[5,4,9,128]{3,2,1,0:T(8,128)S(1)} %constant_dynamic-update-slice_fusion.125, ...), kind=kLoop, calls=%fused_computation.377 | loop fusion | flops 163840 | bytes 753664 | tf_op jit(solution)/shard_map/add | solution.py:237
  (164 shorter events, 4.4 us)
Async XLA Ops:
  0.6 7.4 %copy-start.1 = (f32[9,4,8,128]{3,2,1,0:T(8,128)S(1)}, f32[9,4,8,128]{3,2,1,0:T(8,128)}, u32[]{:S(2)}) copy-start(f32[9,4,8,128]{3,2,1,0:T(8,128)} %param.6) | copy-start | bytes 442372
  1.7 15.6 %collective-permute-start.1 = (f32[5,4,8,3]{3,2,1,0:T(8,128)S(1)}, f32[5,4,8,3]{3,2,1,0:T(8,128)S(1)}, u32[]{:S(2)}, u32[]{:S(2)}) collective-permute-start(f32[5,4,8,3]{3,2,1,0:T(8,128)S(1)} %get-tuple-element.353), channel_id=1, source_target_pairs={{16,0},{17,1},{18,2},{19,3},{20,4},{21,5},{22,6},{23,7},{24,8},{25... | collective-permute-start | bytes 5768 | tf_op jit(solution)/shard_map/ppermute | solution.py:25
  3.0 11.0 %copy-start = (f32[5,4,8,128]{3,2,1,0:T(8,128)S(1)}, f32[5,4,8,128]{3,2,1,0:T(8,128)}, u32[]{:S(2)}) copy-start(f32[5,4,8,128]{3,2,1,0:T(8,128)} %param.5) | copy-start | bytes 245764
  3.0 14.4 %collective-permute-start = (f32[5,4,8,3]{3,2,1,0:T(8,128)S(1)}, f32[5,4,8,3]{3,2,1,0:T(8,128)S(1)}, u32[]{:S(2)}, u32[]{:S(2)}) collective-permute-start(f32[5,4,8,3]{3,2,1,0:T(8,128)S(1)} %get-tuple-element.354), channel_id=1, source_target_pairs={{0,16},{1,17},{2,18},{3,19},{4,20},{5,21},{6,22},{7,23},{8,24},{9,... | collective-permute-start | bytes 5768 | tf_op jit(solution)/shard_map/ppermute | solution.py:22
  8.1 12.6 %collective-permute-start.3 = (f32[9,4,8,3]{3,2,1,0:T(8,128)S(1)}, f32[9,4,8,3]{3,2,1,0:T(8,128)S(1)}, u32[]{:S(2)}, u32[]{:S(2)}) collective-permute-start(f32[9,4,8,3]{3,2,1,0:T(8,128)S(1)} %get-tuple-element.329), channel_id=1, source_target_pairs={{16,0},{17,1},{18,2},{19,3},{20,4},{21,5},{22,6},{23,7},{24,8},{25... | collective-permute-start | bytes 10376 | tf_op jit(solution)/shard_map/ppermute | solution.py:25
  9.4 15.5 %collective-permute-start.2 = (f32[9,4,8,3]{3,2,1,0:T(8,128)S(1)}, f32[9,4,8,3]{3,2,1,0:T(8,128)S(1)}, u32[]{:S(2)}, u32[]{:S(2)}) collective-permute-start(f32[9,4,8,3]{3,2,1,0:T(8,128)S(1)} %get-tuple-element.328), channel_id=1, source_target_pairs={{0,16},{1,17},{2,18},{3,19},{4,20},{5,21},{6,22},{7,23},{8,24},{9,... | collective-permute-start | bytes 10376 | tf_op jit(solution)/shard_map/ppermute | solution.py:22
  14.0 17.6 %collective-permute-start.6 = (f32[5,4,3,128]{3,2,1,0:T(4,128)S(1)}, f32[5,4,3,128]{3,2,1,0:T(4,128)S(1)}, u32[]{:S(2)}, u32[]{:S(2)}) collective-permute-start(f32[5,4,3,128]{3,2,1,0:T(4,128)S(1)} %get-tuple-element.355), channel_id=1, source_target_pairs={{4,0},{8,4},{12,8},{5,1},{9,5},{13,9},{6,2},{10,6},{14,10},{7,3},{... | collective-permute-start | bytes 92168 | tf_op jit(solution)/shard_map/ppermute | solution.py:25
  15.9 0.7 %copy-start.4 = (s32[128]{0:T(128)S(1)}, s32[128]{0:T(128)}, u32[]{:S(2)}) copy-start(s32[128]{0:T(128)} %param.8) | copy-start | bytes 1540
  16.6 0.7 %copy-start.2 = (f32[4,8,128]{2,1,0:T(8,128)S(1)}, f32[4,8,128]{2,1,0:T(8,128)}, u32[]{:S(2)}) copy-start(f32[4,8,128]{2,1,0:T(8,128)} %param.7) | copy-start | bytes 49156
  17.3 16.0 %collective-permute-start.4 = (f32[8,4,3,128]{3,2,1,0:T(4,128)S(1)}, f32[8,4,3,128]{3,2,1,0:T(4,128)S(1)}, u32[]{:S(2)}, u32[]{:S(2)}) collective-permute-start(f32[8,4,3,128]{3,2,1,0:T(4,128)S(1)} %pad_maximum_fusion.11), channel_id=1, source_target_pairs={{0,16},{16,0},{1,17},{17,1},{2,18},{18,2},{3,19},{19,3},{4,20},{20... | collective-permute-start | bytes 147464 | tf_op jit(solution)/shard_map/ppermute | solution.py:12
  17.4 18.3 %collective-permute-start.5 = (f32[5,4,3,128]{3,2,1,0:T(4,128)S(1)}, f32[5,4,3,128]{3,2,1,0:T(4,128)S(1)}, u32[]{:S(2)}, u32[]{:S(2)}) collective-permute-start(f32[5,4,3,128]{3,2,1,0:T(4,128)S(1)} %get-tuple-element.356), channel_id=1, source_target_pairs={{0,4},{4,8},{8,12},{1,5},{5,9},{9,13},{2,6},{6,10},{10,14},{3,7},{... | collective-permute-start | bytes 92168 | tf_op jit(solution)/shard_map/ppermute | solution.py:22
  20.7 15.9 %collective-permute-start.7 = (f32[9,4,3,128]{3,2,1,0:T(4,128)S(1)}, f32[9,4,3,128]{3,2,1,0:T(4,128)S(1)}, u32[]{:S(2)}, u32[]{:S(2)}) collective-permute-start(f32[9,4,3,128]{3,2,1,0:T(4,128)S(1)} %get-tuple-element.332), channel_id=1, source_target_pairs={{0,4},{4,8},{8,12},{1,5},{5,9},{9,13},{2,6},{6,10},{10,14},{3,7},{... | collective-permute-start | bytes 165896 | tf_op jit(solution)/shard_map/ppermute | solution.py:22
  25.0 15.0 %collective-permute-start.8 = (f32[9,4,3,128]{3,2,1,0:T(4,128)S(1)}, f32[9,4,3,128]{3,2,1,0:T(4,128)S(1)}, u32[]{:S(2)}, u32[]{:S(2)}) collective-permute-start(f32[9,4,3,128]{3,2,1,0:T(4,128)S(1)} %get-tuple-element.333), channel_id=1, source_target_pairs={{4,0},{8,4},{12,8},{5,1},{9,5},{13,9},{6,2},{10,6},{14,10},{7,3},{... | collective-permute-start | bytes 165896 | tf_op jit(solution)/shard_map/ppermute | solution.py:25
  31.6 11.6 %collective-permute-start.9 = (f32[5,3,8,128]{3,2,1,0:T(8,128)S(1)}, f32[5,3,8,128]{3,2,1,0:T(8,128)S(1)}, u32[]{:S(2)}, u32[]{:S(2)}) collective-permute-start(f32[5,3,8,128]{3,2,1,0:T(8,128)S(1)} %get-tuple-element.361), channel_id=1, source_target_pairs={{0,1},{1,2},{2,3},{3,0},{4,5},{5,6},{6,7},{7,4},{8,9},{9,10},{10,1... | collective-permute-start | bytes 184328 | tf_op jit(solution)/shard_map/ppermute | solution.py:22
  33.3 10.0 %collective-permute-start.10 = (f32[5,3,8,128]{3,2,1,0:T(8,128)S(1)}, f32[5,3,8,128]{3,2,1,0:T(8,128)S(1)}, u32[]{:S(2)}, u32[]{:S(2)}) collective-permute-start(f32[5,3,8,128]{3,2,1,0:T(8,128)S(1)} %get-tuple-element.360), channel_id=1, source_target_pairs={{1,0},{2,1},{3,2},{0,3},{5,4},{6,5},{7,6},{4,7},{9,8},{10,9},{11,1... | collective-permute-start | bytes 184328 | tf_op jit(solution)/shard_map/ppermute | solution.py:25
  35.7 0.7 %copy-start.3 = (f32[5]{0:T(128)S(1)}, f32[5]{0:T(128)}, u32[]{:S(2)}) copy-start(f32[5]{0:T(128)} %constant.200.clone) | copy-start | bytes 64
  35.7 7.8 %collective-permute-start.11 = (f32[9,3,8,128]{3,2,1,0:T(8,128)S(1)}, f32[9,3,8,128]{3,2,1,0:T(8,128)S(1)}, u32[]{:S(2)}, u32[]{:S(2)}) collective-permute-start(f32[9,3,8,128]{3,2,1,0:T(8,128)S(1)} %get-tuple-element.335), channel_id=1, source_target_pairs={{0,1},{1,2},{2,3},{3,0},{4,5},{5,6},{6,7},{7,4},{8,9},{9,10},{10,1... | collective-permute-start | bytes 331784 | tf_op jit(solution)/shard_map/ppermute | solution.py:22
  36.6 8.0 %collective-permute-start.12 = (f32[9,3,8,128]{3,2,1,0:T(8,128)S(1)}, f32[9,3,8,128]{3,2,1,0:T(8,128)S(1)}, u32[]{:S(2)}, u32[]{:S(2)}) collective-permute-start(f32[9,3,8,128]{3,2,1,0:T(8,128)S(1)} %get-tuple-element.334), channel_id=1, source_target_pairs={{1,0},{2,1},{3,2},{0,3},{5,4},{6,5},{7,6},{4,7},{9,8},{10,9},{11,1... | collective-permute-start | bytes 331784 | tf_op jit(solution)/shard_map/ppermute | solution.py:25
where the time goes:
time: 47.9 us; the launch traced here: 47.5 us
  starting transfers between devices  29.3 us (61%)
  other arithmetic  11.2 us (23%)
  local copies, waits for them, and re-layouts  3.89 us (8%)
  between operations  1.75 us (4%)
  waiting for transfers between devices  1.37 us (3%)
    ppermute x6, starting transfers between devices, padded(): lax.ppermute(lax.slice_in_dim(block, block.shape[dim] - width, None, axis...  18.5 us
    ppermute x6, starting transfers between devices, padded(): lax.ppermute(lax.slice_in_dim(block, 0, width, axis=dim), axis, backward)  10.8 us
    unnamed x100, other arithmetic  5.45 us
    add x3, other arithmetic, interface_flux(): combined = weno_side(upwind[0:5]) + weno_side(downwind[5:0:-1])  2.2 us
    unnamed x14, local copies, waits for them, and re-layouts  1.93 us
    another operation x21, other arithmetic, project_left(): jnp.stack([sum((matrix[member][second] * vector[second] for second in ran...  1.12 us
    ppermute x6, waiting for transfers between devices, padded(): lax.ppermute(lax.slice_in_dim(block, 0, width, axis=dim), axis, backward)  1.08 us
    slice x3, local copies, waits for them, and re-layouts, padded(): lax.slice_in_dim(block, 0, width, axis=dim)  1.07 us
  transfers between devices with their start and end apart: 13, of which 2 were waited for; matrix products, arithmetic and copies ran while one was open for 20% of the time, Pallas kernels for 0%

commit v1 on v0

--- a/solution.py
+++ b/solution.py
@@ -6,10 +6,6 @@
 GAMMA = 1.4
 WENO_EPS = 1e-06
 STEP_SIZE = 0.08
-
-
-def from_partner(x, axis, bit):
-    return lax.ppermute(x, axis, [(i, i ^ 1 << bit) for i in range(lax.axis_size(axis))])
 
 
 def padded(block, sides, width, periodic):
@@ -204,24 +200,15 @@
     at_wall = lax.axis_index("gy") == 0
     at_top = lax.axis_index("gy") == lax.axis_size("gy") - 1
     mirrored = jnp.concatenate([conserved[:, :, 2::-1, :], metrics[3:6, :, 2::-1, :]], axis=0)
-    for bit_number in range(lax.axis_size("gx").bit_length() - 1):
-        mirrored = from_partner(mirrored, "gx", bit_number)
+    count = lax.axis_size("gx")
+    mirrored = lax.ppermute(mirrored, "gx", [(i, count - 1 - i) for i in range(count)])
     mirrored = mirrored[..., ::-1]
-    stream_flow, stream_metric = (
-        padded(conserved, (("gx", 3),), 3, False),
-        padded(metrics, (("gx", 3),), 3, False),
-    )
-    normal_flow, normal_metric = (
-        padded(conserved, (("gy", 2),), 3, False),
-        padded(metrics, (("gy", 2),), 3, False),
-    )
-    span_flow, span_metric = (
-        padded(conserved, (("gz", 1),), 3, True),
-        padded(metrics, (("gz", 1),), 3, True),
-    )
-    stream_row = stream_metric[0:3]
-    normal_row = normal_metric[3:6]
-    span_row = span_metric[6:9]
+    stream = padded(jnp.concatenate([conserved, metrics[0:3]], axis=0), (("gx", 3),), 3, False)
+    normal = padded(jnp.concatenate([conserved, metrics[3:6]], axis=0), (("gy", 2),), 3, False)
+    span = padded(jnp.concatenate([conserved, metrics[6:9]], axis=0), (("gz", 1),), 3, True)
+    stream_flow, stream_row = stream[0:5], stream[5:8]
+    normal_flow, normal_row = normal[0:5], normal[5:8]
+    span_flow, span_row = span[0:5], span[5:8]
     stream_flow = fix_ends(stream_flow, at_inflow, at_outflow)
     stream_row = fix_ends(stream_row, at_inflow, at_outflow)
     momentum_sign = jnp.array([1.0, -1.0, -1.0, -1.0, 1.0], dtype=jnp.float32)[:, None, None, None]

time: 47.9 us -> 33 us (0.69)
  the two profiles are of different devices: /device:TPU:0 before, /device:TPU:1 now
where the time goes in v1:
time: 33 us; the launch traced here: 32.6 us
  starting transfers between devices  15.9 us (48%)
  other arithmetic  11.4 us (35%)
  local copies, waits for them, and re-layouts  3.57 us (11%)
  between operations  1.69 us (5%)
    ppermute x3, starting transfers between devices, padded(): lax.ppermute(lax.slice_in_dim(block, block.shape[dim] - width, None, axis...  10.5 us
    unnamed x100, other arithmetic  5.45 us
    ppermute x3, starting transfers between devices, padded(): lax.ppermute(lax.slice_in_dim(block, 0, width, axis=dim), axis, backward)  5.3 us
    add x3, other arithmetic, interface_flux(): combined = weno_side(upwind[0:5]) + weno_side(downwind[5:0:-1])  2.2 us
    unnamed x12, local copies, waits for them, and re-layouts  1.23 us
    another operation x21, other arithmetic, project_left(): jnp.stack([sum((matrix[member][second] * vector[second] for second in ran...  1.12 us
    slice x1, local copies, waits for them, and re-layouts, local(): metrics[0:3]  0.89 us
    add x1, other arithmetic, local(): return (conserved + STEP_SIZE * time_rate, time_rate)  0.76 us
  transfers between devices with their start and end apart: 7, of which 0 were waited for; matrix products, arithmetic and copies ran while one was open for 29% of the time, Pallas kernels for 0%

profile of v1, /device:TPU:1, one launch (start us, length us, event | category | flops | bytes accessed | tf_op | source)
XLA Modules:
  0.0 32.6 jit_solution(12134740979248576491)
XLA Ops:
  0.6 0.9 %fusion.193 = (f32[3,4,8,128]{3,2,1,0:T(8,128)S(1)}, f32[3,4,8,128]{3,2,1,0:T(8,128)S(1)}, f32[3,4,8,128]{3,2,1,0:T(8,128)S(1)}) fusion(f32[9,4,8,128]{3,2,1,0:T(8,128)} %param.6), kind=kLoop, calls=%fused_computation.683 | loop fusion | bytes 294912 | tf_op jit(solution)/shard_map/slice | solution.py:206
  1.5 0.1 pad_maximum_fusion.7
  1.6 1.3 %collective-permute-start.1 = (f32[8,4,8,3]{3,2,1,0:T(8,128)S(1)}, f32[8,4,8,3]{3,2,1,0:T(8,128)S(1)}, u32[]{:S(2)}, u32[]{:S(2)}) collective-permute-start(f32[8,4,8,3]{3,2,1,0:T(8,128)S(1)} %get-tuple-element.341), channel_id=1, source_target_pairs={{16,0},{17,1},{18,2},{19,3},{20,4},{21,5},{22,6},{23,7},{24,8},{25... | collective-permute-start | bytes 9224 | tf_op jit(solution)/shard_map/ppermute | solution.py:21
  2.9 4.0 %collective-permute-start = (f32[8,4,8,3]{3,2,1,0:T(8,128)S(1)}, f32[8,4,8,3]{3,2,1,0:T(8,128)S(1)}, u32[]{:S(2)}, u32[]{:S(2)}) collective-permute-start(f32[8,4,8,3]{3,2,1,0:T(8,128)S(1)} %get-tuple-element.342), channel_id=1, source_target_pairs={{0,16},{1,17},{2,18},{3,19},{4,20},{5,21},{6,22},{7,23},{8,24},{9,... | collective-permute-start | bytes 9224 | tf_op jit(solution)/shard_map/ppermute | solution.py:18
  7.0 5.2 %collective-permute-start.3 = (f32[8,4,3,128]{3,2,1,0:T(4,128)S(1)}, f32[8,4,3,128]{3,2,1,0:T(4,128)S(1)}, u32[]{:S(2)}, u32[]{:S(2)}) collective-permute-start(f32[8,4,3,128]{3,2,1,0:T(4,128)S(1)} %get-tuple-element.352), channel_id=1, source_target_pairs={{0,4},{4,8},{8,12},{1,5},{5,9},{9,13},{2,6},{6,10},{10,14},{3,7},{... | collective-permute-start | bytes 147464 | tf_op jit(solution)/shard_map/ppermute | solution.py:18
  12.3 0.7 %slice-done = f32[5,4,3,128]{3,2,1,0:T(4,128)S(1)} async-done(((f32[5,4,8,128]{3,2,1,0:T(8,128)}), f32[5,4,3,128]{3,2,1,0:T(4,128)S(1)}, s32[]{:S(2)}) %slice-start) | async-done | bytes 30744 | tf_op jit(solution)/shard_map/slice | solution.py:202
  13.0 0.1 rev.4
  13.1 0.1 collective-permute-start.2
  13.2 1.9 %collective-permute-start.4 = (f32[8,4,3,128]{3,2,1,0:T(4,128)S(1)}, f32[8,4,3,128]{3,2,1,0:T(4,128)S(1)}, u32[]{:S(2)}, u32[]{:S(2)}) collective-permute-start(f32[8,4,3,128]{3,2,1,0:T(4,128)S(1)} %get-tuple-element.351), channel_id=1, source_target_pairs={{4,0},{8,4},{12,8},{5,1},{9,5},{13,9},{6,2},{10,6},{14,10},{7,3},{... | collective-permute-start | bytes 147464 | tf_op jit(solution)/shard_map/ppermute | solution.py:21
  15.1 0.2 slice_reduce_fusion.1
  15.4 0.2 slice_reduce_fusion.3
  15.6 0.7 %copy-done.3 = f32[4,8,128]{2,1,0:T(8,128)S(1)} copy-done((f32[4,8,128]{2,1,0:T(8,128)S(1)}, f32[4,8,128]{2,1,0:T(8,128)}, u32[]{:S(2)}) %copy-start.3) | copy-done | bytes 16408
  16.3 1.3 %collective-permute-start.5 = (f32[8,3,8,128]{3,2,1,0:T(8,128)S(1)}, f32[8,3,8,128]{3,2,1,0:T(8,128)S(1)}, u32[]{:S(2)}, u32[]{:S(2)}) collective-permute-start(f32[8,3,8,128]{3,2,1,0:T(8,128)S(1)} %get-tuple-element.356), channel_id=1, source_target_pairs={{0,1},{1,2},{2,3},{3,0},{4,5},{5,6},{6,7},{7,4},{8,9},{9,10},{10,1... | collective-permute-start | bytes 294920 | tf_op jit(solution)/shard_map/ppermute | solution.py:18
  17.6 0.1 slice_select_fusion
  17.7 2.1 %collective-permute-start.6 = (f32[8,3,8,128]{3,2,1,0:T(8,128)S(1)}, f32[8,3,8,128]{3,2,1,0:T(8,128)S(1)}, u32[]{:S(2)}, u32[]{:S(2)}) collective-permute-start(f32[8,3,8,128]{3,2,1,0:T(8,128)S(1)} %get-tuple-element.355), channel_id=1, source_target_pairs={{1,0},{2,1},{3,2},{0,3},{5,4},{6,5},{7,6},{4,7},{9,8},{10,9},{11,1... | collective-permute-start | bytes 294920 | tf_op jit(solution)/shard_map/ppermute | solution.py:21
  19.8 0.1 slice_select_fusion.1
  19.9 0.1 pad_maximum_fusion.3
  20.0 0.1 slice_select_fusion.2
  20.1 0.1 slice_select_fusion.3
  20.2 0.1 fusion.17
  20.3 0.1 multiply_reduce_fusion.6
  20.5 0.1 fusion.1
  20.6 0.1 constant_dynamic-update-slice_fusion.9
  20.8 0.1 constant_dynamic-update-slice_fusion.29
  20.9 0.1 constant_dynamic-update-slice_fusion.49
  21.1 0.1 constant_dynamic-update-slice_fusion.19
  21.2 0.1 constant_dynamic-update-slice_fusion.59
  21.4 0.2 constant_dynamic-update-slice_fusion.44
  21.5 0.1 constant_dynamic-update-slice_fusion.4
  21.6 0.2 constant_dynamic-update-slice_fusion.24
  21.8 0.1 slice_maximum_fusion.5
  22.0 0.1 constant_dynamic-update-slice_fusion.7
  22.7 0.2 constant_dynamic-update-slice_fusion.43
  22.8 0.1 constant_dynamic-update-slice_fusion.3
  22.9 0.2 constant_dynamic-update-slice_fusion.52
  23.1 0.1 constant_dynamic-update-slice_fusion.2
  23.2 0.1 constant_dynamic-update-slice_fusion.1
  23.3 0.1 constant_dynamic-update-slice_fusion
  23.5 0.2 constant_dynamic-update-slice_fusion.41
  23.6 0.2 constant_dynamic-update-slice_fusion.40
  23.8 0.2 constant_dynamic-update-slice_fusion.23
  23.9 0.2 constant_dynamic-update-slice_fusion.22
  24.1 0.2 constant_dynamic-update-slice_fusion.21
  24.3 0.2 constant_dynamic-update-slice_fusion.20
  24.4 0.8 %divide_add_fusion.1 = f32[5,4,8,129]{3,2,1,0:T(8,128)S(1)} fusion(f32[5,4,8,129]{3,2,1,0:T(8,128)S(1)} %get-tuple-element.218, f32[5,4,8,129]{3,2,1,0:T(8,128)S(1)} %get-tuple-element.217, f32[5,4,8,129]{3,2,1,0:T(8,128)S(1)} %get-tuple-element.212, f32[5,4,8,129]{3,2,1,0:T(8,128)S(1)} %get-tuple-element.211, f32[5,4,8,129]{3,2,1,0:T(8,128)S(1)} %get-tuple-element.206, ...), kind=kLoop, calls=%fused_computation.329 | loop fusion | flops 3034080 | bytes 1089792 | tf_op jit(solution)/shard_map/add | solution.py:171
  25.5 0.1 slice.1108
  25.6 0.5 %copy-done.4 = f32[5]{0:T(128)S(1)} copy-done((f32[5]{0:T(128)S(1)}, f32[5]{0:T(128)}, u32[]{:S(2)}) %copy-start.4) | copy-done | bytes 44
  26.2 0.1 slice_select_fusion.5
  26.3 0.1 slice.1127
  26.7 0.1 constant_dynamic-update-slice_fusion.74
  27.0 0.1 constant_dynamic-update-slice_fusion.109
  27.1 0.1 constant_dynamic-update-slice_fusion.89
  27.3 0.1 constant_dynamic-update-slice_fusion.72
  28.0 0.1 constant_dynamic-update-slice_fusion.108
  28.1 0.1 constant_dynamic-update-slice_fusion.117
  28.3 0.1 constant_dynamic-update-slice_fusion.106
  28.3 0.1 constant_dynamic-update-slice_fusion.105
  28.4 0.1 constant_dynamic-update-slice_fusion.88
  28.5 0.1 constant_dynamic-update-slice_fusion.87
  28.6 0.1 constant_dynamic-update-slice_fusion.85
  28.6 0.8 %divide_add_fusion = f32[5,4,9,128]{3,2,1,0:T(8,128)S(1)} fusion(f32[5,4,9,128]{3,2,1,0:T(8,128)S(1)} %get-tuple-element.239, f32[5,4,9,128]{3,2,1,0:T(8,128)S(1)} %get-tuple-element.238, f32[5,4,9,128]{3,2,1,0:T(8,128)S(1)} %get-tuple-element.233, f32[5,4,9,128]{3,2,1,0:T(8,128)S(1)} %get-tuple-element.232, f32[5,4,9,128]{3,2,1,0:T(8,128)S(1)} %get-tuple-element.227, ...), kind=kLoop, calls=%fused_computation.322 | loop fusion | flops 3386880 | bytes 1216512 | tf_op jit(solution)/shard_map/add | solution.py:171
  29.9 0.1 constant_dynamic-update-slice_fusion.139
  31.1 0.5 %divide_add_fusion.2 = f32[5,5,8,128]{3,2,1,0:T(8,128)S(1)} fusion(f32[5,5,8,128]{3,2,1,0:T(8,128)S(1)} %get-tuple-element.269, f32[5,5,8,128]{3,2,1,0:T(8,128)S(1)} %get-tuple-element.268, f32[5,5,8,128]{3,2,1,0:T(8,128)S(1)} %get-tuple-element.263, f32[5,5,8,128]{3,2,1,0:T(8,128)S(1)} %get-tuple-element.262, f32[5,5,8,128]{3,2,1,0:T(8,128)S(1)} %get-tuple-element.257, ...), kind=kLoop, calls=%fused_computation.346 | loop fusion | flops 3763200 | bytes 1351680 | tf_op jit(solution)/shard_map/add | solution.py:171
  31.8 0.8 %multiply_add_fusion = (f32[5,4,8,128]{3,2,1,0:T(8,128)}, f32[5,4,8,128]{3,2,1,0:T(8,128)}) fusion(f32[5,4,8,128]{3,2,1,0:T(8,128)S(1)} %copy-done.1, f32[5,5,8,128]{3,2,1,0:T(8,128)S(1)} %constant_dynamic-update-slice_fusion.190, f32[5,4,9,128]{3,2,1,0:T(8,128)S(1)} %constant_dynamic-update-slice_fusion.125, ...), kind=kLoop, calls=%fused_computation.381 | loop fusion | flops 163840 | bytes 753664 | tf_op jit(solution)/shard_map/add | solution.py:224
  (149 shorter events, 4.0 us)
Async XLA Ops:
  0.6 0.9 %copy-start = (f32[5,4,8,128]{3,2,1,0:T(8,128)S(1)}, f32[5,4,8,128]{3,2,1,0:T(8,128)}, u32[]{:S(2)}) copy-start(f32[5,4,8,128]{3,2,1,0:T(8,128)} %param.5) | copy-start | bytes 245764
  1.6 14.7 %collective-permute-start.1 = (f32[8,4,8,3]{3,2,1,0:T(8,128)S(1)}, f32[8,4,8,3]{3,2,1,0:T(8,128)S(1)}, u32[]{:S(2)}, u32[]{:S(2)}) collective-permute-start(f32[8,4,8,3]{3,2,1,0:T(8,128)S(1)} %get-tuple-element.341), channel_id=1, source_target_pairs={{16,0},{17,1},{18,2},{19,3},{20,4},{21,5},{22,6},{23,7},{24,8},{25... | collective-permute-start | bytes 9224 | tf_op jit(solution)/shard_map/ppermute | solution.py:21
  2.9 14.7 %collective-permute-start = (f32[8,4,8,3]{3,2,1,0:T(8,128)S(1)}, f32[8,4,8,3]{3,2,1,0:T(8,128)S(1)}, u32[]{:S(2)}, u32[]{:S(2)}) collective-permute-start(f32[8,4,8,3]{3,2,1,0:T(8,128)S(1)} %get-tuple-element.342), channel_id=1, source_target_pairs={{0,16},{1,17},{2,18},{3,19},{4,20},{5,21},{6,22},{7,23},{8,24},{9,... | collective-permute-start | bytes 9224 | tf_op jit(solution)/shard_map/ppermute | solution.py:18
  6.9 5.3 %copy-start.2 = (f32[9,4,8,128]{3,2,1,0:T(8,128)S(1)}, f32[9,4,8,128]{3,2,1,0:T(8,128)}, u32[]{:S(2)}) copy-start(f32[9,4,8,128]{3,2,1,0:T(8,128)} %param.6) | copy-start | bytes 442372
  7.0 18.6 %collective-permute-start.3 = (f32[8,4,3,128]{3,2,1,0:T(4,128)S(1)}, f32[8,4,3,128]{3,2,1,0:T(4,128)S(1)}, u32[]{:S(2)}, u32[]{:S(2)}) collective-permute-start(f32[8,4,3,128]{3,2,1,0:T(4,128)S(1)} %get-tuple-element.352), channel_id=1, source_target_pairs={{0,4},{4,8},{8,12},{1,5},{5,9},{9,13},{2,6},{6,10},{10,14},{3,7},{... | collective-permute-start | bytes 147464 | tf_op jit(solution)/shard_map/ppermute | solution.py:18
  12.2 0.8 %slice-start = ((f32[5,4,8,128]{3,2,1,0:T(8,128)}), f32[5,4,3,128]{3,2,1,0:T(4,128)S(1)}, s32[]{:S(2)}) async-start(f32[5,4,8,128]{3,2,1,0:T(8,128)} %param.5), calls=%async_computation | async-start | bytes 81920 | tf_op jit(solution)/shard_map/slice | solution.py:202
  13.0 2.1 %copy-start.1 = (f32[5,4,8,128]{3,2,1,0:T(8,128)S(1)}, f32[5,4,8,128]{3,2,1,0:T(8,128)}, u32[]{:S(2)}) copy-start(f32[5,4,8,128]{3,2,1,0:T(8,128)} %param.5) | copy-start | bytes 245764
  13.1 12.4 %collective-permute-start.2 = (f32[8,4,3,128]{3,2,1,0:T(4,128)S(1)}, f32[8,4,3,128]{3,2,1,0:T(4,128)S(1)}, u32[]{:S(2)}, u32[]{:S(2)}) collective-permute-start(f32[8,4,3,128]{3,2,1,0:T(4,128)S(1)} %pad_maximum_fusion.16), channel_id=1, source_target_pairs={{0,16},{16,0},{1,17},{17,1},{2,18},{18,2},{3,19},{19,3},{4,20},{20... | collective-permute-start | bytes 147464 | tf_op jit(solution)/shard_map/ppermute | solution.py:204
  13.2 2.1 %copy-start.5 = (s32[128]{0:T(128)S(1)}, s32[128]{0:T(128)}, u32[]{:S(2)}) copy-start(s32[128]{0:T(128)} %param.8) | copy-start | bytes 1540
  13.2 12.2 %collective-permute-start.4 = (f32[8,4,3,128]{3,2,1,0:T(4,128)S(1)}, f32[8,4,3,128]{3,2,1,0:T(4,128)S(1)}, u32[]{:S(2)}, u32[]{:S(2)}) collective-permute-start(f32[8,4,3,128]{3,2,1,0:T(4,128)S(1)} %get-tuple-element.351), channel_id=1, source_target_pairs={{4,0},{8,4},{12,8},{5,1},{9,5},{13,9},{6,2},{10,6},{14,10},{7,3},{... | collective-permute-start | bytes 147464 | tf_op jit(solution)/shard_map/ppermute | solution.py:21
  15.6 0.7 %copy-start.3 = (f32[4,8,128]{2,1,0:T(8,128)S(1)}, f32[4,8,128]{2,1,0:T(8,128)}, u32[]{:S(2)}) copy-start(f32[4,8,128]{2,1,0:T(8,128)} %param.7) | copy-start | bytes 49156
  16.3 13.4 %collective-permute-start.5 = (f32[8,3,8,128]{3,2,1,0:T(8,128)S(1)}, f32[8,3,8,128]{3,2,1,0:T(8,128)S(1)}, u32[]{:S(2)}, u32[]{:S(2)}) collective-permute-start(f32[8,3,8,128]{3,2,1,0:T(8,128)S(1)} %get-tuple-element.356), channel_id=1, source_target_pairs={{0,1},{1,2},{2,3},{3,0},{4,5},{5,6},{6,7},{7,4},{8,9},{9,10},{10,1... | collective-permute-start | bytes 294920 | tf_op jit(solution)/shard_map/ppermute | solution.py:18
  17.7 12.0 %collective-permute-start.6 = (f32[8,3,8,128]{3,2,1,0:T(8,128)S(1)}, f32[8,3,8,128]{3,2,1,0:T(8,128)S(1)}, u32[]{:S(2)}, u32[]{:S(2)}) collective-permute-start(f32[8,3,8,128]{3,2,1,0:T(8,128)S(1)} %get-tuple-element.355), channel_id=1, source_target_pairs={{1,0},{2,1},{3,2},{0,3},{5,4},{6,5},{7,6},{4,7},{9,8},{10,9},{11,1... | collective-permute-start | bytes 294920 | tf_op jit(solution)/shard_map/ppermute | solution.py:21
  25.5 0.7 %copy-start.4 = (f32[5]{0:T(128)S(1)}, f32[5]{0:T(128)}, u32[]{:S(2)}) copy-start(f32[5]{0:T(128)} %constant.200.clone) | copy-start | bytes 64
